TPU v7x, 32 devices: a whole 2x2x4 slice. The times are simulated.
32 devices in a mesh: row: 8 (over y, x, core), col: 4 (over z).
Axes of the slice: x: 2, y: 2, z: 4, core: 2. Of those that a mesh axis runs over, the one named last changes fastest.
Arguments:
- amplitudes: float32 [512, 32, 32, 32], P('col', 'row'), may hold values from -6 to 6
- integrals: float32 [1024, 16384], P('col', 'row'), may hold values from -0.1875 to 0.1875
- occ_energy: float32 [32], replicated, may hold values from -2 to -0.5
- vir_energy: float32 [512], replicated, may hold values from 0.3 to 3
Outputs:
- residual: float32 [16384, 16384], P('col', 'row')
All inputs are finite; a program needn't handle non-finite values.
Results may differ from a plain program's by a relative error of at most 0.00007.
Values sent between devices are 32-bit elements; how exact they have to be, the bound alone decides.
A program may use at most 192 MiB of HBM per device.

v0:
```python
import jax
import jax.numpy as jnp
from jax import lax
from jax.experimental import pallas as pl
from jax.experimental.pallas import tpu as pltpu
from jax.sharding import PartitionSpec as P


CUTS = (0, 4, 6, 7, 8)
A_CUTS = 4
W_CUTS = 4
LANES = 128
PAD = 8
GROUP = 8


def masks(size):
    return [1 << j for j in range(size.bit_length() - 1)]


def split(x):
    high = x.astype(jnp.bfloat16)
    return high, (x - high.astype(jnp.float32)).astype(jnp.bfloat16)


def across(index, bit):
    return index + bit - 2 * bit * (index // bit % 2)


def doubling(me, bits):
    held, flows, partners = [me], [], [across(me, bit) for bit in bits]
    for s, bit in enumerate(bits):
        for j, x in enumerate(list(held)):
            flows.append((s, j))
            held.append(across(x, bit))
    return partners, flows, held


def gather_kernel(
    rows_size, parts, amp_ref, w_ref, vir_ref, down_ref, along_ref, high_ref, low_ref, wide_ref, row_ref, col_ref,
    land, mixed, high, low, own_w, row_gap, col_gap, send, recv, swap_send, swap_recv, w_send, w_recv, local
):
    row, col = lax.axis_index("row"), lax.axis_index("col")
    own, depth, virtuals = amp_ref.shape
    occupied = own * rows_size
    cut = high.shape[1]
    cuts = depth // cut
    w_rows = w_ref.shape[0]
    w_width = wide_ref.shape[1] // W_CUTS

    def chip_bits(device):
        chip = masks(rows_size)[1:]
        odd = device % 2
        return [a + odd * (b - a) for a, b in zip(chip, chip[::-1])]

    sibling = across(row, 1)
    partners, flows, held = doubling(row, chip_bits(row))
    sibling_held = doubling(sibling, chip_bits(sibling))[2]
    w_partners, w_flows, w_held = doubling(col, masks(parts)[::-1])

    barrier = pltpu.get_barrier_semaphore()
    for device in partners + [sibling]:
        pl.semaphore_signal(barrier, inc=1, device_id=(device, col), device_id_type=pl.DeviceIdType.MESH)
    for device in w_partners:
        pl.semaphore_signal(barrier, inc=1, device_id=(row, device), device_id_type=pl.DeviceIdType.MESH)
    pl.semaphore_wait(barrier, len(partners) + 1 + len(w_partners))

    def part(ref, j):
        return ref.at[:, pl.ds(pl.multiple_of(j * cut, cut), cut), :]

    def remote(source, target, send_sem, recv_sem, device):
        return pltpu.make_async_remote_copy(
            src_ref=source, dst_ref=target, send_sem=send_sem, recv_sem=recv_sem,
            device_id=device, device_id_type=pl.DeviceIdType.MESH,
        )

    def flow(j, e):
        s, q = flows[e]
        source = amp_ref if q == 0 else land.at[held[q]]
        return remote(part(source, j), part(land.at[held[q]], j), send.at[j, e], recv.at[j, e], (partners[s], col))

    def arrival(j, e):
        block = part(land.at[held[e + 1]], j)
        return remote(block, block, send.at[j, e], recv.at[j, e], (sibling, col))

    def across_chip(j, q):
        source = amp_ref if q == 0 else land.at[held[q]]
        return remote(part(source, j), part(land.at[held[q]], j), swap_send.at[j, q], swap_recv.at[j, q], (sibling, col))

    def chip_arrival(j, q):
        block = part(land.at[sibling_held[q]], j)
        return remote(block, block, swap_send.at[j, q], swap_recv.at[j, q], (sibling, col))

    def w_span(k):
        return pl.ds(pl.multiple_of(k * w_width, w_width), w_width)

    def w_block(k, q):
        return wide_ref.at[pl.ds(pl.multiple_of(w_held[q] * w_rows, w_rows), w_rows), w_span(k)]

    def w_flow(k, e):
        s, q = w_flows[e]
        source = w_ref.at[:, w_span(k)] if q == 0 else w_block(k, q)
        return remote(source, w_block(k, q), w_send.at[k, e], w_recv.at[k, e], (row, w_partners[s]))

    def w_arrival(k, e):
        block = w_block(k, e + 1)
        return remote(block, block, w_send.at[k, e], w_recv.at[k, e], (row, w_partners[0]))

    def issue(j):
        for e, (s, q) in enumerate(flows):
            if q == 0:
                flow(j, e).start()
        across_chip(j, 0).start()

    issue(0)
    for s in range(len(w_partners)):
        for k in range(W_CUTS):
            for e, (t, q) in enumerate(w_flows):
                if q == 0 and t == s:
                    w_flow(k, e).start()
        if s == 0 and cuts > 1:
            issue(1)
    mine = pltpu.make_async_copy(amp_ref, land.at[row], local.at[0])
    mine.start()
    w_in = pltpu.make_async_copy(w_ref.at[:, pl.ds(0, W_CUTS * w_width)], own_w, local.at[1])
    w_in.start()
    mine.wait()
    w_in.wait()
    w_out = pltpu.make_async_copy(
        own_w, wide_ref.at[pl.ds(pl.multiple_of(col * w_rows, w_rows), w_rows), :], local.at[1]
    )
    w_out.start()

    blocks, stride = cut // LANES, occupied + PAD
    w_relayed = sorted({q - 1 for _, q in w_flows if q})

    def place(device, j):
        for i in range(own):
            for block in range(blocks):
                x = land[device, i, pl.ds(pl.multiple_of(j * cut + block * LANES, LANES), LANES), :]
                mixed[block, pl.ds(device * own + i, virtuals, stride=stride), :] = jnp.swapaxes(x, 0, 1)

    def store(j):
        span = pl.ds(pl.multiple_of(j * cut, cut), cut)
        return [
            pltpu.make_async_copy(high, high_ref.at[:, span], local.at[2]),
            pltpu.make_async_copy(low, low_ref.at[:, span], local.at[3]),
        ]

    gap_copies = [
        pltpu.make_async_copy(row_gap, row_ref, local.at[4]),
        pltpu.make_async_copy(col_gap, col_ref, local.at[5]),
    ]

    def gaps():
        @pl.loop(0, virtuals)
        def _(a):
            rows = pl.ds(pl.multiple_of(a * occupied, occupied), occupied)
            row_gap[rows, :] = vir_ref[col * virtuals + a] - down_ref[...]

        columns = col_gap.shape[1]
        per = LANES // occupied
        place_of = lax.broadcasted_iota(jnp.int32, (8, LANES), 1)

        @pl.loop(0, columns // LANES)
        def _(n):
            first = row * (columns // occupied) + n * per
            value = jnp.full((8, LANES), vir_ref[first], jnp.float32)
            for v in range(1, per):
                value = jnp.where(place_of >= v * occupied, vir_ref[first + v], value)
            col_gap[:, pl.ds(pl.multiple_of(n * LANES, LANES), LANES)] = value - along_ref[...]

        for copy in gap_copies:
            copy.start()

    relayed = sorted({q - 1 for _, q in flows if q})

    def forward(j):
        for e in relayed:
            arrival(j, e).wait_recv()
            for f, (t, p) in enumerate(flows):
                if p == e + 1:
                    flow(j, f).start()
            across_chip(j, e + 1).start()

        @pl.when(j + 2 < cuts)
        def _():
            issue(j + 2)

    forward(0)
    gaps()

    @pl.loop(0, cuts)
    def _(j):
        @pl.when(j + 1 < cuts)
        def _():
            forward(j + 1)

        place(row, j)
        for e in relayed:
            place(held[e + 1], j)
        for n in range(2):
            k = 2 * j + n

            @pl.when(k < W_CUTS)
            def _(k=k):
                for e in w_relayed:
                    w_arrival(k, e).wait_recv()
                    for f, (t, p) in enumerate(w_flows):
                        if p == e + 1:
                            w_flow(k, f).start()
        for e in range(len(flows)):
            if e not in relayed:
                arrival(j, e).wait_recv()
                across_chip(j, e + 1).start()
                place(held[e + 1], j)
        for q in range(len(held)):
            chip_arrival(j, q).wait_recv()
            place(sibling_held[q], j)

        @pl.when(j > 0)
        def _():
            for copy in store(j):
                copy.wait()

        for block in range(blocks):
            lanes = pl.ds(block * LANES, LANES)

            @pl.loop(0, virtuals // GROUP)
            def _(g):
                for n in range(GROUP):
                    a = g * GROUP + n
                    rows = pl.ds(pl.multiple_of(a * occupied, occupied), occupied)
                    x = mixed[block, pl.ds(pl.multiple_of(a * stride, 8), occupied), :]
                    high[rows, lanes], low[rows, lanes] = split(x)

        for copy in store(j):
            copy.start()

    for copy in store(cuts - 1):
        copy.wait()
    w_out.wait()
    for copy in gap_copies:
        copy.wait()
    for k in range(W_CUTS):
        for e in range(len(w_flows)):
            if e not in w_relayed:
                w_arrival(k, e).wait_recv()
    for j in range(cuts):
        for e in range(len(flows)):
            flow(j, e).wait_send()
        for q in range(len(held)):
            across_chip(j, q).wait_send()
    for k in range(W_CUTS):
        for e in range(len(w_flows)):
            w_flow(k, e).wait_send()


def gather(amplitudes, integrals, occ_energy, vir_energy, width):
    own, depth, virtuals = amplitudes.shape
    rows_size, parts = lax.axis_size("row"), lax.axis_size("col")
    occupied = own * rows_size
    cut = depth // A_CUTS
    flows, held, w_flows = rows_size // 2 - 1, rows_size // 2, parts - 1
    terms = jax.ShapeDtypeStruct((occupied * virtuals, depth), jnp.bfloat16)
    wide = jax.ShapeDtypeStruct((parts * integrals.shape[0], width), jnp.float32)
    down = jax.ShapeDtypeStruct((occupied * virtuals, LANES), jnp.float32)
    along = jax.ShapeDtypeStruct((8, integrals.shape[1]), jnp.float32)
    sent = 4 * (amplitudes.size * flows + parts * integrals.shape[0] * width)
    dma = pltpu.SemaphoreType.DMA
    return pl.pallas_call(
        lambda *refs: gather_kernel(rows_size, parts, *refs),
        in_specs=[pl.BlockSpec(memory_space=pl.ANY)] * 2
        + [pl.BlockSpec(memory_space=pltpu.SMEM)] + [pl.BlockSpec(memory_space=pltpu.VMEM)] * 2,
        out_specs=[pl.BlockSpec(memory_space=pl.ANY)] * 5,
        out_shape=[terms, terms, wide, down, along],
        scratch_shapes=[
            pltpu.VMEM((rows_size, own, depth, virtuals), jnp.float32),
            pltpu.VMEM((cut // LANES, virtuals * (occupied + PAD), LANES), jnp.float32),
            pltpu.VMEM((occupied * virtuals, cut), jnp.bfloat16),
            pltpu.VMEM((occupied * virtuals, cut), jnp.bfloat16),
            pltpu.VMEM((integrals.shape[0], width), jnp.float32),
            pltpu.VMEM(down.shape, jnp.float32),
            pltpu.VMEM(along.shape, jnp.float32),
            dma((A_CUTS, flows)), dma((A_CUTS, flows)),
            dma((A_CUTS, held)), dma((A_CUTS, held)),
            dma((W_CUTS, w_flows)), dma((W_CUTS, w_flows)),
            dma((6,)),
        ],
        compiler_params=pltpu.CompilerParams(
            collective_id=0, has_side_effects=True, vmem_limit_bytes=60 * 1024 * 1024
        ),
        cost_estimate=pl.CostEstimate(flops=0, bytes_accessed=sent * 8, transcendentals=0),
        name="gather",
    )(
        amplitudes,
        integrals,
        vir_energy,
        jnp.broadcast_to(occ_energy[:, None], (occupied, LANES)),
        jnp.broadcast_to(jnp.tile(occ_energy, LANES // occupied)[None, :], (8, LANES)),
    )


def product_kernel(groups, parts, steps, aliased, where_ref, *refs):
    count, halves = groups * parts, len(steps)
    pieces, refs = refs[:count], refs[count:]
    terms, refs = refs[: 2 * halves], refs[2 * halves :]
    row_ref, col_ref = refs[:2]
    out_ref, w_ref = refs[2 + aliased :]
    depth, width = pieces[0].shape
    whole = parts * depth
    m = pl.program_id(0)

    @pl.when(m == 0)
    def _():
        for j, piece in enumerate(pieces):
            start = pl.multiple_of(where_ref[j % parts] * depth, depth)
            lanes = pl.ds(j // parts * width, width)
            w_high, w_low = split(piece[...])
            w_ref[pl.ds(start, depth), lanes] = w_high
            w_ref[pl.ds(start + whole, depth), lanes] = w_high
            w_ref[pl.ds(start + 2 * whole, depth), lanes] = w_low

    def multiply(high_ref, low_ref):
        high = high_ref[...]
        both = jnp.concatenate([high, low_ref[...], high], axis=1)
        total = jnp.dot(both, w_ref[...], preferred_element_type=jnp.float32)
        out_ref[...] = total / (row_ref[:, :1] + col_ref[:1, :])

    if halves == 1:
        multiply(*terms)
    else:
        stop = 0
        for h, step in enumerate(steps):
            start, stop = stop, stop + step
            pl.when((m >= start) & (m < stop))(lambda h=h: multiply(terms[2 * h], terms[2 * h + 1]))


def product(where, chunks, halves, row_gap, col_gap, out, shape, top, start):
    groups, parts = len(chunks), len(chunks[0])
    depth, width = chunks[0][0].shape
    total = groups * width
    whole = halves[0][0].shape[1]
    tile = min(512 if total > 256 else 1024, halves[0][0].shape[0])
    steps = [high.shape[0] // tile for high, _ in halves]
    rows = sum(steps) * tile
    first, chunk = top // tile, start // total
    aliased = 0 if out is None else 1
    in_specs = [pl.BlockSpec((depth, width), lambda m, s: (0, 0), pipeline_mode=pl.Buffered(1))] * (groups * parts)
    before = 0
    for step in steps:
        index = lambda m, s, before=before, step=step: (jnp.clip(m - before, 0, step - 1), 0)
        in_specs += [pl.BlockSpec((tile, whole), index)] * 2
        before += step
    in_specs += [pl.BlockSpec((tile, LANES), lambda m, s: (m + first, 0))]
    in_specs += [pl.BlockSpec((8, total), lambda m, s: (0, chunk))]
    operands = [where, *(piece for pieces in chunks for piece in pieces)]
    operands += [term for half in halves for term in half] + [row_gap, col_gap]
    if aliased:
        in_specs += [pl.BlockSpec(memory_space=pl.ANY)]
        operands += [out]
    return pl.pallas_call(
        lambda *refs: product_kernel(groups, parts, steps, aliased, *refs),
        grid_spec=pltpu.PrefetchScalarGridSpec(
            num_scalar_prefetch=1,
            grid=(sum(steps),),
            in_specs=in_specs,
            out_specs=pl.BlockSpec((tile, total), lambda m, s: (m + first, chunk)),
            scratch_shapes=[pltpu.VMEM((3 * whole, total), jnp.bfloat16)],
        ),
        out_shape=jax.ShapeDtypeStruct(shape, jnp.float32),
        input_output_aliases={len(operands) - 1: 0} if aliased else {},
        cost_estimate=pl.CostEstimate(
            flops=6 * rows * total * whole, bytes_accessed=4 * rows * (total + whole), transcendentals=0
        ),
        name="product",
    )(*operands)


def swap(x, axis, size, step):
    return lax.ppermute(x, axis, [(j, step(j)) for j in range(size)])


def double(piece, axis, size, steps):
    held = [piece]
    for step in steps:
        for x in list(held):
            held.append(swap(x, axis, size, step))
    return held


def direct(piece, axis, size, offsets):
    return [piece] + [swap(piece, axis, size, lambda j, m=m: j ^ m) for m in offsets[1:]]


def body(amplitudes, integrals, occ_energy, vir_energy):
    virtuals, own = amplitudes.shape[:2]
    rows_size, parts = lax.axis_size("row"), lax.axis_size("col")
    occupied = own * rows_size
    whole = amplitudes.shape[2] * amplitudes.shape[3]
    columns = integrals.shape[1]
    height = virtuals * occupied
    col = lax.axis_index("col")

    starts = [columns * cut // CUTS[-1] for cut in CUTS]
    own_pieces = [integrals[:, a:b] for a, b in zip(starts, starts[1:])]
    order = masks(parts)[::-1]
    steps = [lambda j, bit=bit: j ^ bit for bit in order]
    offsets = [0]
    for bit in order:
        offsets += [m ^ bit for m in offsets]
    where = jnp.stack([col ^ m for m in offsets]).astype(jnp.int32)

    turned = jnp.transpose(amplitudes, (1, 2, 3, 0)).reshape(own, whole, virtuals)
    high, low, wide, row_gap, col_gap = gather(turned, integrals, occ_energy, vir_energy, starts[1])
    half = (high, low)
    chunk1 = double(own_pieces[1], "col", parts, steps)
    chunk2 = direct(own_pieces[2], "col", parts, offsets)
    chunk3 = direct(own_pieces[3], "col", parts, offsets)

    def block(out, where, chunks, start):
        return product(where, chunks, [half], row_gap, col_gap, out, (height, columns), 0, start)

    plain = jnp.zeros((1,), jnp.int32)
    out = block(None, plain, [[wide]], starts[0])
    out = block(out, where, [chunk1], starts[1])
    out = block(out, where, [chunk2], starts[2])
    return block(out, where, [chunk3], starts[3])


def solution(mesh):
    in_specs = (P("col", "row", None, None), P("col", "row"), P(), P())
    out_specs = P("col", "row")
    return jax.shard_map(body, mesh=mesh, in_specs=in_specs, out_specs=out_specs, check_vma=False)
```

profile of v0, /device:TPU:0, one launch (start us, length us, event | category | flops | bytes accessed | tf_op | source)
XLA Modules:
  0.0 203.0 jit_solution(2916806944897864357)
XLA Ops:
  0.0 1.1 slice.11.refs_1_
  1.1 0.0 copy-start
  1.1 4.1 %collective-permute-start.6 = (f32[256,512]{1,0:T(8,128)S(1)}, f32[256,512]{1,0:T(8,128)S(1)}, u32[]{:S(2)}, u32[]{:S(2)}) collective-permute-start(f32[256,512]{1,0:T(8,128)S(1)} %slice.11.refs_1_), channel_id=1, source_target_pairs={{0,2},{1,3},{2,0},{3,1},{4,6},{5,7},{6,4},{7,5},{8,10},{9,11},{10,... | collective-permute-start | bytes 1572872 | tf_op jit(solution)/shard_map/ppermute | solution.py:381
  5.2 1.6 collective-permute-start.7
  6.8 1.1 fusion
  7.9 0.0 copy-start.2
  7.9 0.0 copy-start.1
  7.9 0.4 collective-permute-start.3
  8.3 0.2 collective-permute-start.4
  8.5 3.9 %collective-permute-start.5 = (f32[256,256]{1,0:T(8,128)S(1)}, f32[256,256]{1,0:T(8,128)S(1)}, u32[]{:S(2)}, u32[]{:S(2)}) collective-permute-start(f32[256,256]{1,0:T(8,128)S(1)} %get-tuple-element.15.refs_1_), channel_id=1, source_target_pairs={{0,3},{1,2},{2,1},{3,0},{4,7},{5,6},{6,5},{7,4},{8,11},{9,10},{10,... | collective-permute-start | bytes 786440 | tf_op jit(solution)/shard_map/ppermute | solution.py:381
  12.3 0.7 tile.2
  13.0 0.1 broadcast_in_dim.14
  13.1 1.3 broadcast_in_dim.6.refs_3_
  14.4 0.6 broadcast_in_dim.15.refs_4_
  15.0 98.9 %gather.1 = (bf16[4096,1024]{1,0:T(8,128)(2,1)}, bf16[4096,1024]{1,0:T(8,128)(2,1)}, f32[1024,1024]{1,0:T(8,128)}, f32[4096,128]{1,0:T(8,128)}, f32[8,2048]{1,0:T(8,128)}) custom-call(f32[4,1024,128]{2,1,0:T(8,128)} %bitcast.7, f32[256,2048]{1,0:T(8,128)} %refs_1_.1, f32[512]{0:T(512)} %refs_2_.1, f32[32,128]{1,0:T(8,128)} %broadcast_in_dim.6.refs_3_, ...), custom_call_target="tpu_custom_call" | custom-call | bytes 83886080 | tf_op jit(solution)/shard_map/gather/pallas_call | solution.py:271
  113.9 0.0 collective-permute-done.6.refs_2_
  113.9 0.0 copy-start.3
  113.9 1.6 collective-permute-start.8
  115.5 33.1 %product.4.refs_9_ = f32[4096,2048]{1,0:T(8,128)} custom-call(s32[1]{0:T(128)} %constant.4.clone.1.refs_0_, f32[1024,1024]{1,0:T(8,128)} %get-tuple-element.14.refs_1_, bf16[4096,1024]{1,0:T(8,128)(2,1)} %get-tuple-element.10.refs_2_.refs_5_, bf16[4096,1024]{1,0:T(8,128)(2,1)} %get-tuple-element.11.refs_3_.refs_6_, ...), custom_call_target="tpu_custom_call" | custom-call | flops 25769803776 | bytes 33554432 | tf_op jit(solution)/shard_map/product/pallas_call | solution.py:362
  148.7 0.0 copy-done
  148.7 0.0 copy-done.2
  148.7 0.0 copy-done.3
  148.7 0.6 pad_add_fusion.refs_0_
  149.3 0.0 collective-permute-done.7.refs_3_
  149.3 0.0 copy-start.4
  149.3 2.0 collective-permute-start
  151.2 0.0 collective-permute-done.8.refs_4_
  151.2 0.0 copy-start.5
  151.2 0.1 collective-permute-start.1
  151.3 0.0 copy-done.4
  151.3 0.7 copy-done.5
  152.0 19.7 %product.5.refs_9_ = f32[4096,2048]{1,0:T(8,128)} custom-call(s32[4]{0:T(128)} %pad_add_fusion.refs_0_, f32[256,512]{1,0:T(8,128)} %copy-done, f32[256,512]{1,0:T(8,128)} %copy-done.3, f32[256,512]{1,0:T(8,128)} %copy-done.4, f32[256,512]{1,0:T(8,128)} %copy-done.5, ...), custom_call_target="tpu_custom_call", output_to_operand_aliasing={{}: (9, {})} | custom-call | flops 12884901888 | bytes 25165824 | tf_op jit(solution)/shard_map/product/pallas_call | solution.py:362
  171.7 0.0 collective-permute-done.3.refs_2_
  171.7 0.0 copy-done.1
  171.7 0.0 copy-start.6
  171.7 1.7 collective-permute-start.2
  173.4 0.0 collective-permute-done.4.refs_3_
  173.4 0.0 copy-start.7
  173.4 0.0 collective-permute-done.5.refs_4_
  173.4 0.0 copy-done.6
  173.4 0.7 copy-done.7
  174.1 0.0 copy-start.8
  174.1 0.7 copy-done.8
  174.8 13.3 %product.6.refs_9_ = f32[4096,2048]{1,0:T(8,128)} custom-call(s32[4]{0:T(128)} %pad_add_fusion.refs_0_, f32[256,256]{1,0:T(8,128)} %copy-done.2, f32[256,256]{1,0:T(8,128)} %copy-done.6, f32[256,256]{1,0:T(8,128)} %copy-done.7, f32[256,256]{1,0:T(8,128)} %copy-done.8, ...), custom_call_target="tpu_custom_call", output_to_operand_aliasing={{}: (9, {})} | custom-call | flops 6442450944 | bytes 20971520 | tf_op jit(solution)/shard_map/product/pallas_call | solution.py:362
  188.1 0.0 collective-permute-done.refs_2_
  188.2 0.0 copy-start.9
  188.2 0.0 collective-permute-done.1.refs_3_
  188.2 0.0 copy-start.10
  188.2 0.0 collective-permute-done.2.refs_4_
  188.2 0.7 copy-done.9
  188.9 0.1 copy-done.10
  188.9 0.0 copy-start.11
  188.9 0.7 copy-done.11
  189.7 13.3 %product.7 = f32[4096,2048]{1,0:T(8,128)} custom-call(s32[4]{0:T(128)} %pad_add_fusion.refs_0_, f32[256,256]{1,0:T(8,128)} %copy-done.1, f32[256,256]{1,0:T(8,128)} %copy-done.9, f32[256,256]{1,0:T(8,128)} %copy-done.10, f32[256,256]{1,0:T(8,128)} %copy-done.11, ...), custom_call_target="tpu_custom_call", output_to_operand_aliasing={{}: (9, {})} | custom-call | flops 6442450944 | bytes 20971520 | tf_op jit(solution)/shard_map/product/pallas_call | solution.py:362
Async XLA Ops:
  1.1 147.6 %copy-start = (f32[256,512]{1,0:T(8,128)}, f32[256,512]{1,0:T(8,128)S(1)}, u32[]{:S(2)}) copy-start(f32[256,512]{1,0:T(8,128)S(1)} %slice.11.refs_1_) | copy-start | bytes 1572868
  1.1 112.8 %collective-permute-start.6 = (f32[256,512]{1,0:T(8,128)S(1)}, f32[256,512]{1,0:T(8,128)S(1)}, u32[]{:S(2)}, u32[]{:S(2)}) collective-permute-start(f32[256,512]{1,0:T(8,128)S(1)} %slice.11.refs_1_), channel_id=1, source_target_pairs={{0,2},{1,3},{2,0},{3,1},{4,6},{5,7},{6,4},{7,5},{8,10},{9,11},{10,... | collective-permute-start | bytes 1572872 | tf_op jit(solution)/shard_map/ppermute | solution.py:381
  5.2 144.0 %collective-permute-start.7 = (f32[256,512]{1,0:T(8,128)S(1)}, f32[256,512]{1,0:T(8,128)S(1)}, u32[]{:S(2)}, u32[]{:S(2)}) collective-permute-start(f32[256,512]{1,0:T(8,128)S(1)} %slice.11.refs_1_), channel_id=1, source_target_pairs={{0,1},{1,0},{2,3},{3,2},{4,5},{5,4},{6,7},{7,6},{8,9},{9,8},{10,11... | collective-permute-start | bytes 1572872 | tf_op jit(solution)/shard_map/ppermute | solution.py:381
  7.9 140.8 %copy-start.2 = (f32[256,256]{1,0:T(8,128)}, f32[256,256]{1,0:T(8,128)S(1)}, u32[]{:S(2)}) copy-start(f32[256,256]{1,0:T(8,128)S(1)} %get-tuple-element.15.refs_1_) | copy-start | bytes 786436
  7.9 163.8 %copy-start.1 = (f32[256,256]{1,0:T(8,128)}, f32[256,256]{1,0:T(8,128)S(1)}, u32[]{:S(2)}) copy-start(f32[256,256]{1,0:T(8,128)S(1)} %get-tuple-element.16.refs_1_) | copy-start | bytes 786436
  7.9 163.8 %collective-permute-start.3 = (f32[256,256]{1,0:T(8,128)S(1)}, f32[256,256]{1,0:T(8,128)S(1)}, u32[]{:S(2)}, u32[]{:S(2)}) collective-permute-start(f32[256,256]{1,0:T(8,128)S(1)} %get-tuple-element.15.refs_1_), channel_id=1, source_target_pairs={{0,2},{1,3},{2,0},{3,1},{4,6},{5,7},{6,4},{7,5},{8,10},{9,11},{10,... | collective-permute-start | bytes 786440 | tf_op jit(solution)/shard_map/ppermute | solution.py:381
  8.3 165.1 %collective-permute-start.4 = (f32[256,256]{1,0:T(8,128)S(1)}, f32[256,256]{1,0:T(8,128)S(1)}, u32[]{:S(2)}, u32[]{:S(2)}) collective-permute-start(f32[256,256]{1,0:T(8,128)S(1)} %get-tuple-element.15.refs_1_), channel_id=1, source_target_pairs={{0,1},{1,0},{2,3},{3,2},{4,5},{5,4},{6,7},{7,6},{8,9},{9,8},{10,11... | collective-permute-start | bytes 786440 | tf_op jit(solution)/shard_map/ppermute | solution.py:381
  8.5 164.9 %collective-permute-start.5 = (f32[256,256]{1,0:T(8,128)S(1)}, f32[256,256]{1,0:T(8,128)S(1)}, u32[]{:S(2)}, u32[]{:S(2)}) collective-permute-start(f32[256,256]{1,0:T(8,128)S(1)} %get-tuple-element.15.refs_1_), channel_id=1, source_target_pairs={{0,3},{1,2},{2,1},{3,0},{4,7},{5,6},{6,5},{7,4},{8,11},{9,10},{10,... | collective-permute-start | bytes 786440 | tf_op jit(solution)/shard_map/ppermute | solution.py:381
  113.9 34.8 %copy-start.3 = (f32[256,512]{1,0:T(8,128)}, f32[256,512]{1,0:T(8,128)S(1)}, u32[]{:S(2)}) copy-start(f32[256,512]{1,0:T(8,128)S(1)} %collective-permute-done.6.refs_2_) | copy-start | bytes 1572868
  113.9 37.3 %collective-permute-start.8 = (f32[256,512]{1,0:T(8,128)S(1)}, f32[256,512]{1,0:T(8,128)S(1)}, u32[]{:S(2)}, u32[]{:S(2)}) collective-permute-start(f32[256,512]{1,0:T(8,128)S(1)} %collective-permute-done.6.refs_2_), channel_id=1, source_target_pairs={{0,1},{1,0},{2,3},{3,2},{4,5},{5,4},{6,7},{7,6},{8,9},{9,8},{10,11... | collective-permute-start | bytes 1572872 | tf_op jit(solution)/shard_map/ppermute | solution.py:381
  149.3 2.1 %copy-start.4 = (f32[256,512]{1,0:T(8,128)}, f32[256,512]{1,0:T(8,128)S(1)}, u32[]{:S(2)}) copy-start(f32[256,512]{1,0:T(8,128)S(1)} %collective-permute-done.7.refs_3_) | copy-start | bytes 1572868
  149.3 38.9 %collective-permute-start = (f32[256,256]{1,0:T(8,128)S(1)}, f32[256,256]{1,0:T(8,128)S(1)}, u32[]{:S(2)}, u32[]{:S(2)}) collective-permute-start(f32[256,256]{1,0:T(8,128)S(1)} %get-tuple-element.16.refs_1_), channel_id=1, source_target_pairs={{0,2},{1,3},{2,0},{3,1},{4,6},{5,7},{6,4},{7,5},{8,10},{9,11},{10,... | collective-permute-start | bytes 786440 | tf_op jit(solution)/shard_map/ppermute | solution.py:381
  151.2 0.8 copy-start.5
  151.2 36.9 %collective-permute-start.1 = (f32[256,256]{1,0:T(8,128)S(1)}, f32[256,256]{1,0:T(8,128)S(1)}, u32[]{:S(2)}, u32[]{:S(2)}) collective-permute-start(f32[256,256]{1,0:T(8,128)S(1)} %get-tuple-element.16.refs_1_), channel_id=1, source_target_pairs={{0,1},{1,0},{2,3},{3,2},{4,5},{5,4},{6,7},{7,6},{8,9},{9,8},{10,11... | collective-permute-start | bytes 786440 | tf_op jit(solution)/shard_map/ppermute | solution.py:381
  171.7 1.7 copy-start.6
  171.7 16.5 %collective-permute-start.2 = (f32[256,256]{1,0:T(8,128)S(1)}, f32[256,256]{1,0:T(8,128)S(1)}, u32[]{:S(2)}, u32[]{:S(2)}) collective-permute-start(f32[256,256]{1,0:T(8,128)S(1)} %get-tuple-element.16.refs_1_), channel_id=1, source_target_pairs={{0,3},{1,2},{2,1},{3,0},{4,7},{5,6},{6,5},{7,4},{8,11},{9,10},{10,... | collective-permute-start | bytes 786440 | tf_op jit(solution)/shard_map/ppermute | solution.py:381
  173.4 0.7 copy-start.7
  174.1 0.7 copy-start.8
  188.2 0.7 copy-start.9
  188.2 0.8 copy-start.10
  188.9 0.7 copy-start.11
where the time goes:
time: 204 us; the launch traced here: 203 us
  Pallas kernels  178 us (87%)
  starting transfers between devices  15.6 us (8%)
  local copies, waits for them, and re-layouts  8.38 us (4%)
    pallas_call x1, Pallas kernels, gather(): pl.pallas_call(lambda *refs: gather_kernel(rows_size, parts, *refs), in_s...  98.9 us
    pallas_call x4, Pallas kernels, product(): pl.pallas_call(lambda *refs: product_kernel(groups, parts, steps, aliased...  79.4 us
    ppermute x9, starting transfers between devices, swap(): return lax.ppermute(x, axis, [(j, step(j)) for j in range(size)])  15.6 us
  transfers between devices with their start and end apart: 9, of which 0 were waited for; matrix products, arithmetic and copies ran while one was open for 2% of the time, Pallas kernels for 81%

commit v1 on v0

--- a/solution.py
+++ b/solution.py
@@ -6,7 +6,7 @@
 from jax.sharding import PartitionSpec as P
 
 
-CUTS = (0, 4, 6, 7, 8)
+CUTS = (0, 4, 6, 8)
 A_CUTS = 4
 W_CUTS = 4
 LANES = 128
@@ -37,7 +37,7 @@
 
 
 def gather_kernel(
-    rows_size, parts, amp_ref, w_ref, vir_ref, down_ref, along_ref, high_ref, low_ref, wide_ref, row_ref, col_ref,
+    rows_size, parts, amp_ref, w_ref, vir_ref, occ_ref, high_ref, low_ref, wide_ref, row_ref, col_ref,
     land, mixed, high, low, own_w, row_gap, col_gap, send, recv, swap_send, swap_recv, w_send, w_recv, local
 ):
     row, col = lax.axis_index("row"), lax.axis_index("col")
@@ -152,11 +152,21 @@
         pltpu.make_async_copy(col_gap, col_ref, local.at[5]),
     ]
 
+    def spread(shape, axis):
+        at = lax.broadcasted_iota(jnp.int32, shape, axis) % occupied
+        value = jnp.full(shape, occ_ref[0], jnp.float32)
+        for i in range(1, occupied):
+            value = jnp.where(at >= i, occ_ref[i], value)
+        return value
+
     def gaps():
+        down = spread((occupied, LANES), 0)
+        along = spread((8, LANES), 1)
+
         @pl.loop(0, virtuals)
         def _(a):
             rows = pl.ds(pl.multiple_of(a * occupied, occupied), occupied)
-            row_gap[rows, :] = vir_ref[col * virtuals + a] - down_ref[...]
+            row_gap[rows, :] = vir_ref[col * virtuals + a] - down
 
         columns = col_gap.shape[1]
         per = LANES // occupied
@@ -168,7 +178,7 @@
             value = jnp.full((8, LANES), vir_ref[first], jnp.float32)
             for v in range(1, per):
                 value = jnp.where(place_of >= v * occupied, vir_ref[first + v], value)
-            col_gap[:, pl.ds(pl.multiple_of(n * LANES, LANES), LANES)] = value - along_ref[...]
+            col_gap[:, pl.ds(pl.multiple_of(n * LANES, LANES), LANES)] = value - along
 
         for copy in gap_copies:
             copy.start()
@@ -271,7 +281,7 @@
     return pl.pallas_call(
         lambda *refs: gather_kernel(rows_size, parts, *refs),
         in_specs=[pl.BlockSpec(memory_space=pl.ANY)] * 2
-        + [pl.BlockSpec(memory_space=pltpu.SMEM)] + [pl.BlockSpec(memory_space=pltpu.VMEM)] * 2,
+        + [pl.BlockSpec(memory_space=pltpu.SMEM)] * 2,
         out_specs=[pl.BlockSpec(memory_space=pl.ANY)] * 5,
         out_shape=[terms, terms, wide, down, along],
         scratch_shapes=[
@@ -296,8 +306,7 @@
         amplitudes,
         integrals,
         vir_energy,
-        jnp.broadcast_to(occ_energy[:, None], (occupied, LANES)),
-        jnp.broadcast_to(jnp.tile(occ_energy, LANES // occupied)[None, :], (8, LANES)),
+        occ_energy,
     )
 
 
@@ -389,10 +398,6 @@
     return held
 
 
-def direct(piece, axis, size, offsets):
-    return [piece] + [swap(piece, axis, size, lambda j, m=m: j ^ m) for m in offsets[1:]]
-
-
 def body(amplitudes, integrals, occ_energy, vir_energy):
     virtuals, own = amplitudes.shape[:2]
     rows_size, parts = lax.axis_size("row"), lax.axis_size("col")
@@ -415,8 +420,7 @@
     high, low, wide, row_gap, col_gap = gather(turned, integrals, occ_energy, vir_energy, starts[1])
     half = (high, low)
     chunk1 = double(own_pieces[1], "col", parts, steps)
-    chunk2 = direct(own_pieces[2], "col", parts, offsets)
-    chunk3 = direct(own_pieces[3], "col", parts, offsets)
+    chunk2 = double(own_pieces[2], "col", parts, steps)
 
     def block(out, where, chunks, start):
         return product(where, chunks, [half], row_gap, col_gap, out, (height, columns), 0, start)
@@ -424,8 +428,7 @@
     plain = jnp.zeros((1,), jnp.int32)
     out = block(None, plain, [[wide]], starts[0])
     out = block(out, where, [chunk1], starts[1])
-    out = block(out, where, [chunk2], starts[2])
-    return block(out, where, [chunk3], starts[3])
+    return block(out, where, [chunk2], starts[2])
 
 
 def solution(mesh):

time: 204 us -> 197 us (0.966)
  starting transfers between devices: 15.6 us -> 8.33 us
  Pallas kernels: 178 us -> 185 us
  local copies, waits for them, and re-layouts: 8.38 us -> 2.91 us
    pallas_call x1, Pallas kernels: 98.9 us -> 112 us  [gather(): pl.pallas_call(lambda *refs: gather_kernel(rows_size, parts, *refs), in_s...]
    ppermute x9 -> x6, starting transfers between devices: 15.6 us -> 8.33 us  [swap(): return lax.ppermute(x, axis, [(j, step(j)) for j in range(size)])]
    pallas_call x4 -> x3, Pallas kernels: 79.4 us -> 72.5 us  [product(): pl.pallas_call(lambda *refs: product_kernel(groups, parts, steps, aliased...]
  transfers between devices with their start and end apart: 9 -> 6, of which waited for: 0 -> 0; matrix products, arithmetic and copies ran while one was open for 2% -> 0% of each run, Pallas kernels for 81% -> 84%
where the time goes in v1:
time: 197 us
  Pallas kernels  185 us (94%)
  starting transfers between devices  8.33 us (4%)
  local copies, waits for them, and re-layouts  2.91 us (1%)
    pallas_call x1, Pallas kernels, gather(): pl.pallas_call(lambda *refs: gather_kernel(rows_size, parts, *refs), in_s...  112 us
    pallas_call x3, Pallas kernels, product(): pl.pallas_call(lambda *refs: product_kernel(groups, parts, steps, aliased...  72.5 us
    ppermute x6, starting transfers between devices, swap(): return lax.ppermute(x, axis, [(j, step(j)) for j in range(size)])  8.33 us
  transfers between devices with their start and end apart: 6, of which 0 were waited for; matrix products, arithmetic and copies ran while one was open for 0% of the time, Pallas kernels for 84%

profile of v1, /device:TPU:0, one launch (start us, length us, event | category | flops | bytes accessed | tf_op | source)
XLA Modules:
  0.0 196.6 jit_solution(9361091694221922620)
XLA Ops:
  0.0 1.3 fusion
  1.3 0.0 copy-start
  1.3 0.0 copy-start.1
  1.3 4.1 %collective-permute-start.3 = (f32[256,512]{1,0:T(8,128)S(1)}, f32[256,512]{1,0:T(8,128)S(1)}, u32[]{:S(2)}, u32[]{:S(2)}) collective-permute-start(f32[256,512]{1,0:T(8,128)S(1)} %get-tuple-element.15.refs_1_), channel_id=1, source_target_pairs={{0,2},{1,3},{2,0},{3,1},{4,6},{5,7},{6,4},{7,5},{8,10},{9,11},{10,... | collective-permute-start | bytes 1572872 | tf_op jit(solution)/shard_map/ppermute | solution.py:390
  5.4 1.6 collective-permute-start.4
  7.0 0.3 collective-permute-start
  7.3 0.2 collective-permute-start.1
  7.5 112.2 %gather.1 = (bf16[4096,1024]{1,0:T(8,128)(2,1)}, bf16[4096,1024]{1,0:T(8,128)(2,1)}, f32[1024,1024]{1,0:T(8,128)}, f32[4096,128]{1,0:T(8,128)}, f32[8,2048]{1,0:T(8,128)}) custom-call(f32[4,1024,128]{2,1,0:T(8,128)} %bitcast.7, f32[256,2048]{1,0:T(8,128)} %refs_1_.1, f32[512]{0:T(512)} %refs_2_.1, f32[32]{0:T(128)} %refs_3_.1), custom_call_target="tpu_custom_call" | custom-call | bytes 83886080 | tf_op jit(solution)/shard_map/gather/pallas_call | solution.py:281
  119.7 0.0 collective-permute-done.3.refs_2_
  119.7 0.0 copy-start.3
  119.7 1.6 collective-permute-start.5
  121.4 33.1 %product.3.refs_9_ = f32[4096,2048]{1,0:T(8,128)} custom-call(s32[1]{0:T(128)} %constant.4.clone.1.refs_0_, f32[1024,1024]{1,0:T(8,128)} %get-tuple-element.14.refs_1_, bf16[4096,1024]{1,0:T(8,128)(2,1)} %get-tuple-element.10.refs_2_.refs_5_, bf16[4096,1024]{1,0:T(8,128)(2,1)} %get-tuple-element.11.refs_3_.refs_6_, ...), custom_call_target="tpu_custom_call" | custom-call | flops 25769803776 | bytes 33554432 | tf_op jit(solution)/shard_map/product/pallas_call | solution.py:371
  154.5 0.0 copy-done
  154.5 0.0 copy-done.1
  154.5 0.0 copy-done.3
  154.5 0.6 pad_add_fusion.refs_0_
  155.1 0.0 collective-permute-done.refs_2_
  155.1 0.0 copy-start.2
  155.1 0.5 collective-permute-start.2
  155.6 0.0 collective-permute-done.4.refs_3_
  155.6 0.0 copy-start.5
  155.6 0.0 collective-permute-done.5.refs_4_
  155.6 0.8 copy-done.5
  156.4 19.7 %product.4.refs_9_ = f32[4096,2048]{1,0:T(8,128)} custom-call(s32[4]{0:T(128)} %pad_add_fusion.refs_0_, f32[256,512]{1,0:T(8,128)} %copy-done.1, f32[256,512]{1,0:T(8,128)} %copy-done.3, f32[256,512]{1,0:T(8,128)} %copy-done.5, f32[256,512]{1,0:T(8,128)} %collective-permute-done.5.refs_4_, ...), custom_call_target="tpu_custom_call", output_to_operand_aliasing={{}: (9, {})} | custom-call | flops 12884901888 | bytes 25165824 | tf_op jit(solution)/shard_map/product/pallas_call | solution.py:371
  176.1 0.0 copy-done.2
  176.1 0.0 collective-permute-done.1.refs_3_
  176.1 0.0 copy-start.4
  176.1 0.0 collective-permute-done.2.refs_4_
  176.1 0.8 copy-done.4
  176.9 19.7 %product.5 = f32[4096,2048]{1,0:T(8,128)} custom-call(s32[4]{0:T(128)} %pad_add_fusion.refs_0_, f32[256,512]{1,0:T(8,128)} %copy-done, f32[256,512]{1,0:T(8,128)} %copy-done.2, f32[256,512]{1,0:T(8,128)} %copy-done.4, f32[256,512]{1,0:T(8,128)} %collective-permute-done.2.refs_4_, ...), custom_call_target="tpu_custom_call", output_to_operand_aliasing={{}: (9, {})} | custom-call | flops 12884901888 | bytes 25165824 | tf_op jit(solution)/shard_map/product/pallas_call | solution.py:371
Async XLA Ops:
  1.3 153.2 %copy-start = (f32[256,512]{1,0:T(8,128)}, f32[256,512]{1,0:T(8,128)S(1)}, u32[]{:S(2)}) copy-start(f32[256,512]{1,0:T(8,128)S(1)} %get-tuple-element.16.refs_1_) | copy-start | bytes 1572868
  1.3 153.2 %copy-start.1 = (f32[256,512]{1,0:T(8,128)}, f32[256,512]{1,0:T(8,128)S(1)}, u32[]{:S(2)}) copy-start(f32[256,512]{1,0:T(8,128)S(1)} %get-tuple-element.15.refs_1_) | copy-start | bytes 1572868
  1.3 118.4 %collective-permute-start.3 = (f32[256,512]{1,0:T(8,128)S(1)}, f32[256,512]{1,0:T(8,128)S(1)}, u32[]{:S(2)}, u32[]{:S(2)}) collective-permute-start(f32[256,512]{1,0:T(8,128)S(1)} %get-tuple-element.15.refs_1_), channel_id=1, source_target_pairs={{0,2},{1,3},{2,0},{3,1},{4,6},{5,7},{6,4},{7,5},{8,10},{9,11},{10,... | collective-permute-start | bytes 1572872 | tf_op jit(solution)/shard_map/ppermute | solution.py:390
  5.4 150.1 %collective-permute-start.4 = (f32[256,512]{1,0:T(8,128)S(1)}, f32[256,512]{1,0:T(8,128)S(1)}, u32[]{:S(2)}, u32[]{:S(2)}) collective-permute-start(f32[256,512]{1,0:T(8,128)S(1)} %get-tuple-element.15.refs_1_), channel_id=1, source_target_pairs={{0,1},{1,0},{2,3},{3,2},{4,5},{5,4},{6,7},{7,6},{8,9},{9,8},{10,11... | collective-permute-start | bytes 1572872 | tf_op jit(solution)/shard_map/ppermute | solution.py:390
  7.0 148.1 %collective-permute-start = (f32[256,512]{1,0:T(8,128)S(1)}, f32[256,512]{1,0:T(8,128)S(1)}, u32[]{:S(2)}, u32[]{:S(2)}) collective-permute-start(f32[256,512]{1,0:T(8,128)S(1)} %get-tuple-element.16.refs_1_), channel_id=1, source_target_pairs={{0,2},{1,3},{2,0},{3,1},{4,6},{5,7},{6,4},{7,5},{8,10},{9,11},{10,... | collective-permute-start | bytes 1572872 | tf_op jit(solution)/shard_map/ppermute | solution.py:390
  7.3 168.7 %collective-permute-start.1 = (f32[256,512]{1,0:T(8,128)S(1)}, f32[256,512]{1,0:T(8,128)S(1)}, u32[]{:S(2)}, u32[]{:S(2)}) collective-permute-start(f32[256,512]{1,0:T(8,128)S(1)} %get-tuple-element.16.refs_1_), channel_id=1, source_target_pairs={{0,1},{1,0},{2,3},{3,2},{4,5},{5,4},{6,7},{7,6},{8,9},{9,8},{10,11... | collective-permute-start | bytes 1572872 | tf_op jit(solution)/shard_map/ppermute | solution.py:390
  119.7 34.8 %copy-start.3 = (f32[256,512]{1,0:T(8,128)}, f32[256,512]{1,0:T(8,128)S(1)}, u32[]{:S(2)}) copy-start(f32[256,512]{1,0:T(8,128)S(1)} %collective-permute-done.3.refs_2_) | copy-start | bytes 1572868
  119.7 35.8 %collective-permute-start.5 = (f32[256,512]{1,0:T(8,128)S(1)}, f32[256,512]{1,0:T(8,128)}, u32[]{:S(2)}, u32[]{:S(2)}) collective-permute-start(f32[256,512]{1,0:T(8,128)S(1)} %collective-permute-done.3.refs_2_), channel_id=1, source_target_pairs={{0,1},{1,0},{2,3},{3,2},{4,5},{5,4},{6,7},{7,6},{8,9},{9,8},{10,11... | collective-permute-start | bytes 1572872 | tf_op jit(solution)/shard_map/ppermute | solution.py:390
  155.1 21.0 %copy-start.2 = (f32[256,512]{1,0:T(8,128)}, f32[256,512]{1,0:T(8,128)S(1)}, u32[]{:S(2)}) copy-start(f32[256,512]{1,0:T(8,128)S(1)} %collective-permute-done.refs_2_) | copy-start | bytes 1572868
  155.1 21.0 %collective-permute-start.2 = (f32[256,512]{1,0:T(8,128)S(1)}, f32[256,512]{1,0:T(8,128)}, u32[]{:S(2)}, u32[]{:S(2)}) collective-permute-start(f32[256,512]{1,0:T(8,128)S(1)} %collective-permute-done.refs_2_), channel_id=1, source_target_pairs={{0,1},{1,0},{2,3},{3,2},{4,5},{5,4},{6,7},{7,6},{8,9},{9,8},{10,11... | collective-permute-start | bytes 1572872 | tf_op jit(solution)/shard_map/ppermute | solution.py:390
  155.6 0.8 copy-start.5
  176.1 0.8 copy-start.4

commit v2 on v1

--- a/solution.py
+++ b/solution.py
@@ -322,8 +322,9 @@
 
     @pl.when(m == 0)
     def _():
+        origin = doubling(lax.axis_index("col"), masks(parts)[::-1])[2] if parts > 1 else [0]
         for j, piece in enumerate(pieces):
-            start = pl.multiple_of(where_ref[j % parts] * depth, depth)
+            start = pl.multiple_of(origin[j % parts] * depth, depth)
             lanes = pl.ds(j // parts * width, width)
             w_high, w_low = split(piece[...])
             w_ref[pl.ds(start, depth), lanes] = w_high
@@ -427,8 +428,8 @@
 
     plain = jnp.zeros((1,), jnp.int32)
     out = block(None, plain, [[wide]], starts[0])
-    out = block(out, where, [chunk1], starts[1])
-    return block(out, where, [chunk2], starts[2])
+    out = block(out, plain, [chunk1], starts[1])
+    return block(out, plain, [chunk2], starts[2])
 
 
 def solution(mesh):

time: 197 us -> 195 us (0.990)
  Pallas kernels: 185 us -> 183 us
where the time goes in v2:
time: 195 us
  Pallas kernels  183 us (94%)
  starting transfers between devices  8.39 us (4%)
  local copies, waits for them, and re-layouts  2.91 us (1%)
    pallas_call x1, Pallas kernels, gather(): pl.pallas_call(lambda *refs: gather_kernel(rows_size, parts, *refs), in_s...  112 us
    pallas_call x3, Pallas kernels, product(): pl.pallas_call(lambda *refs: product_kernel(groups, parts, steps, aliased...  70.9 us
    ppermute x6, starting transfers between devices, swap(): return lax.ppermute(x, axis, [(j, step(j)) for j in range(size)])  8.39 us
  transfers between devices with their start and end apart: 6, of which 0 were waited for; matrix products, arithmetic and copies ran while one was open for 0% of the time, Pallas kernels for 84%

profile of v2, /device:TPU:0, one launch (start us, length us, event | category | flops | bytes accessed | tf_op | source)
XLA Modules:
  0.0 194.5 jit_solution(5163475553323764743)
XLA Ops:
  0.0 1.3 fusion
  1.3 0.0 copy-start
  1.3 0.0 copy-start.1
  1.3 4.1 %collective-permute-start.3 = (f32[256,512]{1,0:T(8,128)S(1)}, f32[256,512]{1,0:T(8,128)S(1)}, u32[]{:S(2)}, u32[]{:S(2)}) collective-permute-start(f32[256,512]{1,0:T(8,128)S(1)} %get-tuple-element.15.refs_1_), channel_id=1, source_target_pairs={{0,2},{1,3},{2,0},{3,1},{4,6},{5,7},{6,4},{7,5},{8,10},{9,11},{10,... | collective-permute-start | bytes 1572872 | tf_op jit(solution)/shard_map/ppermute | solution.py:391
  5.4 1.6 collective-permute-start.4
  7.0 0.3 collective-permute-start
  7.3 0.2 collective-permute-start.1
  7.5 112.2 %gather.1 = (bf16[4096,1024]{1,0:T(8,128)(2,1)}, bf16[4096,1024]{1,0:T(8,128)(2,1)}, f32[1024,1024]{1,0:T(8,128)}, f32[4096,128]{1,0:T(8,128)}, f32[8,2048]{1,0:T(8,128)}) custom-call(f32[4,1024,128]{2,1,0:T(8,128)} %bitcast.3, f32[256,2048]{1,0:T(8,128)} %refs_1_.1, f32[512]{0:T(512)} %refs_2_.1, f32[32]{0:T(128)} %refs_3_.1), custom_call_target="tpu_custom_call" | custom-call | bytes 83886080 | tf_op jit(solution)/shard_map/gather/pallas_call | solution.py:281
  119.7 0.0 collective-permute-done.3.refs_2_
  119.7 0.0 copy-start.4
  119.7 1.6 collective-permute-start.5
  121.4 32.9 %product.3.refs_9_ = f32[4096,2048]{1,0:T(8,128)} custom-call(s32[1]{0:T(128)} %constant.0.clone.1.refs_0_, f32[1024,1024]{1,0:T(8,128)} %get-tuple-element.14.refs_1_, bf16[4096,1024]{1,0:T(8,128)(2,1)} %get-tuple-element.10.refs_2_.refs_5_, bf16[4096,1024]{1,0:T(8,128)(2,1)} %get-tuple-element.11.refs_3_.refs_6_, ...), custom_call_target="tpu_custom_call" | custom-call | flops 25769803776 | bytes 33554432 | tf_op jit(solution)/shard_map/product/pallas_call | solution.py:372
  154.3 0.0 copy-done
  154.3 0.0 copy-done.1
  154.3 0.0 copy-done.4
  154.3 0.0 collective-permute-done.refs_2_
  154.3 0.0 copy-start.2
  154.3 0.5 collective-permute-start.2
  154.8 0.0 collective-permute-done.4.refs_3_
  154.8 0.0 copy-start.5
  154.8 0.0 collective-permute-done.5.refs_4_
  154.8 0.8 copy-done.5
  155.7 19.0 %product.4.refs_9_ = f32[4096,2048]{1,0:T(8,128)} custom-call(s32[1]{0:T(128)} %constant.0.clone.1.refs_0_, f32[256,512]{1,0:T(8,128)} %copy-done.1, f32[256,512]{1,0:T(8,128)} %copy-done.4, f32[256,512]{1,0:T(8,128)} %copy-done.5, f32[256,512]{1,0:T(8,128)} %collective-permute-done.5.refs_4_, ...), custom_call_target="tpu_custom_call", output_to_operand_aliasing={{}: (9, {})} | custom-call | flops 12884901888 | bytes 25165824 | tf_op jit(solution)/shard_map/product/pallas_call | solution.py:372
  174.7 0.0 copy-done.2
  174.7 0.0 collective-permute-done.1.refs_3_
  174.7 0.0 copy-start.3
  174.7 0.0 collective-permute-done.2.refs_4_
  174.7 0.8 copy-done.3
  175.5 19.0 %product.5 = f32[4096,2048]{1,0:T(8,128)} custom-call(s32[1]{0:T(128)} %constant.0.clone.1.refs_0_, f32[256,512]{1,0:T(8,128)} %copy-done, f32[256,512]{1,0:T(8,128)} %copy-done.2, f32[256,512]{1,0:T(8,128)} %copy-done.3, f32[256,512]{1,0:T(8,128)} %collective-permute-done.2.refs_4_, ...), custom_call_target="tpu_custom_call", output_to_operand_aliasing={{}: (9, {})} | custom-call | flops 12884901888 | bytes 25165824 | tf_op jit(solution)/shard_map/product/pallas_call | solution.py:372
Async XLA Ops:
  1.3 153.0 %copy-start = (f32[256,512]{1,0:T(8,128)}, f32[256,512]{1,0:T(8,128)S(1)}, u32[]{:S(2)}) copy-start(f32[256,512]{1,0:T(8,128)S(1)} %get-tuple-element.16.refs_1_) | copy-start | bytes 1572868
  1.3 153.0 %copy-start.1 = (f32[256,512]{1,0:T(8,128)}, f32[256,512]{1,0:T(8,128)S(1)}, u32[]{:S(2)}) copy-start(f32[256,512]{1,0:T(8,128)S(1)} %get-tuple-element.15.refs_1_) | copy-start | bytes 1572868
  1.3 118.4 %collective-permute-start.3 = (f32[256,512]{1,0:T(8,128)S(1)}, f32[256,512]{1,0:T(8,128)S(1)}, u32[]{:S(2)}, u32[]{:S(2)}) collective-permute-start(f32[256,512]{1,0:T(8,128)S(1)} %get-tuple-element.15.refs_1_), channel_id=1, source_target_pairs={{0,2},{1,3},{2,0},{3,1},{4,6},{5,7},{6,4},{7,5},{8,10},{9,11},{10,... | collective-permute-start | bytes 1572872 | tf_op jit(solution)/shard_map/ppermute | solution.py:391
  5.4 149.4 %collective-permute-start.4 = (f32[256,512]{1,0:T(8,128)S(1)}, f32[256,512]{1,0:T(8,128)S(1)}, u32[]{:S(2)}, u32[]{:S(2)}) collective-permute-start(f32[256,512]{1,0:T(8,128)S(1)} %get-tuple-element.15.refs_1_), channel_id=1, source_target_pairs={{0,1},{1,0},{2,3},{3,2},{4,5},{5,4},{6,7},{7,6},{8,9},{9,8},{10,11... | collective-permute-start | bytes 1572872 | tf_op jit(solution)/shard_map/ppermute | solution.py:391
  7.0 147.3 %collective-permute-start = (f32[256,512]{1,0:T(8,128)S(1)}, f32[256,512]{1,0:T(8,128)S(1)}, u32[]{:S(2)}, u32[]{:S(2)}) collective-permute-start(f32[256,512]{1,0:T(8,128)S(1)} %get-tuple-element.16.refs_1_), channel_id=1, source_target_pairs={{0,2},{1,3},{2,0},{3,1},{4,6},{5,7},{6,4},{7,5},{8,10},{9,11},{10,... | collective-permute-start | bytes 1572872 | tf_op jit(solution)/shard_map/ppermute | solution.py:391
  7.3 167.3 %collective-permute-start.1 = (f32[256,512]{1,0:T(8,128)S(1)}, f32[256,512]{1,0:T(8,128)S(1)}, u32[]{:S(2)}, u32[]{:S(2)}) collective-permute-start(f32[256,512]{1,0:T(8,128)S(1)} %get-tuple-element.16.refs_1_), channel_id=1, source_target_pairs={{0,1},{1,0},{2,3},{3,2},{4,5},{5,4},{6,7},{7,6},{8,9},{9,8},{10,11... | collective-permute-start | bytes 1572872 | tf_op jit(solution)/shard_map/ppermute | solution.py:391
  119.7 34.6 %copy-start.4 = (f32[256,512]{1,0:T(8,128)}, f32[256,512]{1,0:T(8,128)S(1)}, u32[]{:S(2)}) copy-start(f32[256,512]{1,0:T(8,128)S(1)} %collective-permute-done.3.refs_2_) | copy-start | bytes 1572868
  119.7 35.1 %collective-permute-start.5 = (f32[256,512]{1,0:T(8,128)S(1)}, f32[256,512]{1,0:T(8,128)}, u32[]{:S(2)}, u32[]{:S(2)}) collective-permute-start(f32[256,512]{1,0:T(8,128)S(1)} %collective-permute-done.3.refs_2_), channel_id=1, source_target_pairs={{0,1},{1,0},{2,3},{3,2},{4,5},{5,4},{6,7},{7,6},{8,9},{9,8},{10,11... | collective-permute-start | bytes 1572872 | tf_op jit(solution)/shard_map/ppermute | solution.py:391
  154.3 20.4 %copy-start.2 = (f32[256,512]{1,0:T(8,128)}, f32[256,512]{1,0:T(8,128)S(1)}, u32[]{:S(2)}) copy-start(f32[256,512]{1,0:T(8,128)S(1)} %collective-permute-done.refs_2_) | copy-start | bytes 1572868
  154.3 20.4 %collective-permute-start.2 = (f32[256,512]{1,0:T(8,128)S(1)}, f32[256,512]{1,0:T(8,128)}, u32[]{:S(2)}, u32[]{:S(2)}) collective-permute-start(f32[256,512]{1,0:T(8,128)S(1)} %collective-permute-done.refs_2_), channel_id=1, source_target_pairs={{0,1},{1,0},{2,3},{3,2},{4,5},{5,4},{6,7},{7,6},{8,9},{9,8},{10,11... | collective-permute-start | bytes 1572872 | tf_op jit(solution)/shard_map/ppermute | solution.py:391
  154.8 0.8 copy-start.5
  174.7 0.8 copy-start.3
